TPU v7x, 32 devices: a whole 2x2x4 slice. The times are simulated.
32 devices in a mesh: dp: 4 (over y, x), expert: 8 (over z, core).
Axes of the slice: x: 2, y: 2, z: 4, core: 2. Of those that a mesh axis runs over, the one named last changes fastest.
Arguments:
- tokens: bfloat16 [4096, 7168], P(('dp', 'expert')), may hold values from -6 to 6
- route_ids: int32 [4096, 8], P(('dp', 'expert')), may hold values from 0 to 255, as said below
- gate_weights: float32 [4096, 8], P(('dp', 'expert')), may hold values from 0.3 to 1.2
- gate_weight: bfloat16 [8, 7168, 1024], P('expert', 'dp'), may hold values from -0.0625 to 0.0625
- up_weight: bfloat16 [8, 7168, 1024], P('expert', 'dp'), may hold values from -0.0625 to 0.0625
- down_weight: bfloat16 [8, 7168, 1024], P('expert', 'dp'), may hold values from -0.1875 to 0.1875
- cotangent: bfloat16 [4096, 7168], P(('dp', 'expert')), may hold values from -3 to 3
Outputs:
- output: bfloat16 [4096, 7168], P(('dp', 'expert'))
- grad_tokens: bfloat16 [4096, 7168], P(('dp', 'expert'))
- grad_gate: bfloat16 [8, 7168, 1024], P('expert', 'dp')
- grad_up: bfloat16 [8, 7168, 1024], P('expert', 'dp')
- grad_down: bfloat16 [8, 7168, 1024], P('expert', 'dp')
Inputs may be any that keep to these rules, and one draw needn't show every extreme that they name: `route_ids`: each token's 8 numbers are different, and at most one of them is below 8. Among the 128 tokens of one device at most 4 name any one number below 8; for each index of dp, one number below 8 is named by exactly 4 tokens of every device with that index.
All inputs are finite; a program needn't handle non-finite values.
Results may differ from a plain program's by a relative error of at most 0.018.
Values may be sent and summed in bfloat16 or wider, within the bound.
No kernel may reach another device: no remote copies, remote signals or barrier semaphores. Data moves between devices by JAX's collectives and lax.ppermute only.
A program may use at most 128 MiB of HBM per device.

v0:
```python
import jax
import jax.numpy as jnp
from jax import lax
from jax.sharding import PartitionSpec as P

CAP = 4


def contract_last(left, right):
    return lax.dot_general(
        left, right, (((1,), (1,)), ((), ())), preferred_element_type=jnp.float32
    )


def contract_first(left, right):
    return lax.dot_general(
        left, right, (((0,), (0,)), ((), ())), preferred_element_type=jnp.float32
    )


def body(tokens, route_ids, gate_weights, gate_weight, up_weight, down_weight, cotangent):
    experts = lax.axis_size("expert")
    gate_mat = gate_weight[0]
    up_mat = up_weight[0]
    down_mat = down_weight[0]
    slice_width = gate_mat.shape[0]
    hidden_units = gate_mat.shape[1]
    labels = jnp.arange(experts, dtype=jnp.int32)
    matches = route_ids[:, :, None] == labels
    chosen = jnp.any(matches, axis=1).astype(jnp.int32)
    gate_of = jnp.sum(jnp.where(matches, gate_weights[:, :, None], 0.0), axis=1)
    ranks = jnp.cumsum(chosen, axis=0) - chosen
    placed = (chosen[:, :, None] == 1) & (ranks[:, :, None] == jnp.arange(CAP, dtype=jnp.int32))
    placer = placed.astype(jnp.bfloat16)
    slot_gate = jnp.sum(jnp.where(placed, gate_of[:, :, None], 0.0), axis=0)
    send_rows = jnp.einsum(
        "tjc,td->jcd", placer, tokens, preferred_element_type=jnp.float32
    ).astype(jnp.bfloat16)
    picked = jnp.einsum("tjc,td->jcd", placer, cotangent, preferred_element_type=jnp.float32)
    send_grads = (slot_gate[:, :, None] * picked).astype(jnp.bfloat16)
    recv_rows, recv_grads = (
        lax.all_to_all(
            lax.all_to_all(send_rows, "dp", split_axis=2, concat_axis=1, tiled=True),
            "expert",
            split_axis=0,
            concat_axis=0,
            tiled=True,
        ),
        lax.all_to_all(
            lax.all_to_all(send_grads, "dp", split_axis=2, concat_axis=1, tiled=True),
            "expert",
            split_axis=0,
            concat_axis=0,
            tiled=True,
        ),
    )
    layout = recv_rows.shape
    row_count = layout[0] * layout[1]
    flat_rows = recv_rows.reshape(row_count, slice_width)
    flat_grads = recv_grads.reshape(row_count, slice_width)
    row_block = flat_rows
    grad_block = flat_grads
    mine = lax.psum_scatter(
        jnp.concatenate(
            [
                jnp.dot(row_block, gate_mat, preferred_element_type=jnp.float32),
                jnp.dot(row_block, up_mat, preferred_element_type=jnp.float32),
                jnp.dot(grad_block, down_mat, preferred_element_type=jnp.float32),
            ],
            axis=1,
        ).astype(jnp.bfloat16),
        "dp",
        scatter_dimension=0,
        tiled=True,
    ).astype(jnp.float32)
    pre_gate = mine[:, :hidden_units]
    pre_up = mine[:, hidden_units : 2 * hidden_units]
    hidden_grad = mine[:, 2 * hidden_units :]
    squash = jax.nn.sigmoid(pre_gate)
    silu_gate = pre_gate * squash
    hidden = (silu_gate * pre_up).astype(jnp.bfloat16)
    gate_grad = (hidden_grad * pre_up * squash * (1.0 + pre_gate * (1.0 - squash))).astype(
        jnp.bfloat16
    )
    up_grad = (hidden_grad * silu_gate).astype(jnp.bfloat16)
    hidden, gate_grad, up_grad = (hidden, gate_grad, up_grad)
    hidden_part = lax.all_gather(hidden, "dp", axis=0, tiled=True)
    gate_part = lax.all_gather(gate_grad, "dp", axis=0, tiled=True)
    up_part = lax.all_gather(up_grad, "dp", axis=0, tiled=True)
    row_block = flat_rows
    grad_block = flat_grads
    out_part = contract_last(hidden_part, down_mat).astype(jnp.bfloat16)
    input_part = (contract_last(gate_part, gate_mat) + contract_last(up_part, up_mat)).astype(
        jnp.bfloat16
    )
    out_rows = out_part
    input_rows = input_part
    gate_total = contract_first(row_block, gate_part)
    up_total = contract_first(row_block, up_part)
    down_total = contract_first(grad_block, hidden_part)
    carry = (out_rows, input_rows, gate_total, up_total, down_total)
    out_rows, input_rows, gate_total, up_total, down_total = carry
    got_out, got_input = (
        lax.all_to_all(
            lax.all_to_all(out_rows.reshape(layout), "dp", split_axis=1, concat_axis=2, tiled=True),
            "expert",
            split_axis=0,
            concat_axis=0,
            tiled=True,
        ),
        lax.all_to_all(
            lax.all_to_all(
                input_rows.reshape(layout), "dp", split_axis=1, concat_axis=2, tiled=True
            ),
            "expert",
            split_axis=0,
            concat_axis=0,
            tiled=True,
        ),
    )
    weighted = slot_gate[:, :, None] * got_out.astype(jnp.float32)
    output = jnp.einsum(
        "tjc,jcd->td", placed.astype(jnp.float32), weighted, precision=lax.Precision.HIGHEST
    ).astype(jnp.bfloat16)
    grad_tokens = jnp.einsum(
        "tjc,jcd->td", placer, got_input, preferred_element_type=jnp.float32
    ).astype(jnp.bfloat16)
    return (
        output,
        grad_tokens,
        gate_total.astype(jnp.bfloat16)[None],
        up_total.astype(jnp.bfloat16)[None],
        down_total.astype(jnp.bfloat16)[None],
    )


def solution(mesh):
    return jax.shard_map(
        body,
        mesh=mesh,
        in_specs=(
            P(("dp", "expert"), None),
            P(("dp", "expert"), None),
            P(("dp", "expert"), None),
            P("expert", "dp", None),
            P("expert", "dp", None),
            P("expert", "dp", None),
            P(("dp", "expert"), None),
        ),
        out_specs=(
            P(("dp", "expert"), None),
            P(("dp", "expert"), None),
            P("expert", "dp", None),
            P("expert", "dp", None),
            P("expert", "dp", None),
        ),
        check_vma=False,
    )
```

profile of v0, /device:TPU:0, one launch (start us, length us, event | category | flops | bytes accessed | tf_op | source)
XLA Modules:
  0.0 243.5 jit_solution(8787925912496322918)
XLA Ops:
  7.2 0.8 fusion.44
  8.7 0.4 convolution_convert_fusion
  9.1 7.2 %copy.72 = bf16[8,4,7168]{0,1,2:T(4,128)(2,1)} copy(bf16[8,4,7168]{2,0,1:T(8,128)(2,1)S(1)} %convolution_convert_fusion) | data formatting | bytes 917504 | tf_op jit(solution)/shard_map/convert_element_type | solution.py:38
  16.3 10.2 %reshape.53 = bf16[4,2,28672]{2,1,0:T(2,128)(2,1)} reshape(bf16[7168,4,8]{2,1,0:T(4,128)(2,1)} %bitcast.83) | data formatting | bytes 917504
  26.5 5.2 %all-to-all-start = ((bf16[4,2,28672]{2,1,0:T(2,128)(2,1)}), bf16[4,2,28672]{2,1,0:T(2,128)(2,1)S(1)}, u32[]{:S(2)}, u32[]{:S(2)}) async-start(bf16[4,2,28672]{2,1,0:T(2,128)(2,1)} %reshape.53), calls=%async_computation | async-start | bytes 917504 | tf_op jit(solution)/shard_map/all_to_all | solution.py:43
  31.8 0.4 fusion.2
  32.2 7.2 %copy.76 = bf16[8,4,7168]{0,1,2:T(4,128)(2,1)} copy(bf16[8,4,7168]{2,0,1:T(8,128)(2,1)S(1)} %fusion.2) | data formatting | bytes 917504 | tf_op jit(solution)/shard_map/convert_element_type | solution.py:40
  39.4 10.1 %reshape.51 = bf16[4,2,28672]{2,1,0:T(2,128)(2,1)} reshape(bf16[7168,4,8]{2,1,0:T(4,128)(2,1)} %bitcast.84) | data formatting | bytes 917504
  49.5 4.2 %all-to-all-start.2 = ((bf16[4,2,28672]{2,1,0:T(2,128)(2,1)}), bf16[4,2,28672]{2,1,0:T(2,128)(2,1)S(1)}, u32[]{:S(2)}, u32[]{:S(2)}) async-start(bf16[4,2,28672]{2,1,0:T(2,128)(2,1)} %reshape.51), calls=%async_computation.2 | async-start | bytes 917504 | tf_op jit(solution)/shard_map/all_to_all | solution.py:50
  53.6 9.8 %reshape.54 = bf16[7168,4,8]{2,1,0:T(4,128)(2,1)} reshape(bf16[4,2,28672]{2,1,0:T(2,128)(2,1)S(1)} %all-to-all-done) | data formatting | bytes 917504
  63.4 8.7 %copy.74 = bf16[8,4,4,1792]{3,0,2,1:T(8,128)(2,1)S(1)} copy(bf16[8,4,4,1792]{0,2,3,1:T(4,128)(2,1)} %bitcast.85) | data formatting | bytes 917504 | tf_op jit(solution)/shard_map/all_to_all | solution.py:43
  72.1 0.8 copy.75
  73.0 4.9 %all-to-all-start.1 = ((bf16[8,16,1792]{2,1,0:T(8,128)(2,1)}), bf16[8,16,1792]{2,1,0:T(8,128)(2,1)S(1)}, u32[]{:S(2)}, u32[]{:S(2)}) async-start(bf16[8,16,1792]{2,1,0:T(8,128)(2,1)} %copy.75), calls=%async_computation.1 | async-start | bytes 917504 | tf_op jit(solution)/shard_map/all_to_all | solution.py:42
  77.9 9.8 %reshape.52 = bf16[7168,4,8]{2,1,0:T(4,128)(2,1)} reshape(bf16[4,2,28672]{2,1,0:T(2,128)(2,1)S(1)} %all-to-all-done.2) | data formatting | bytes 917504
  87.7 8.7 %copy.78 = bf16[8,4,4,1792]{3,0,2,1:T(8,128)(2,1)S(1)} copy(bf16[8,4,4,1792]{0,2,3,1:T(4,128)(2,1)} %bitcast.86) | data formatting | bytes 917504 | tf_op jit(solution)/shard_map/all_to_all | solution.py:50
  96.4 0.8 copy.79
  97.2 5.1 %all-to-all-start.3 = ((bf16[8,16,1792]{2,1,0:T(8,128)(2,1)}), bf16[8,16,1792]{2,1,0:T(8,128)(2,1)S(1)}, u32[]{:S(2)}, u32[]{:S(2)}) async-start(bf16[8,16,1792]{2,1,0:T(8,128)(2,1)} %copy.79), calls=%async_computation.3 | async-start | bytes 917504 | tf_op jit(solution)/shard_map/all_to_all | solution.py:49
  102.3 2.8 %fusion.32 = bf16[128,1024]{1,0:T(8,128)(2,1)S(1)} fusion(bf16[128,1792]{1,0:T(8,128)(2,1)S(1)} %bitcast.87, bf16[1,1792,1024]{2,1,0:T(8,128)(2,1)} %param.11), kind=kOutput, calls=%fused_computation.31 | convolution fusion | flops 469893120 | bytes 4390912 | tf_op jit(solution)/shard_map/dot_general | solution.py:67
  105.5 0.6 fusion.29
  106.1 10.1 %all-to-all-done.3 = bf16[8,16,1792]{2,1,0:T(8,128)(2,1)S(1)} async-done(((bf16[8,16,1792]{2,1,0:T(8,128)(2,1)}), bf16[8,16,1792]{2,1,0:T(8,128)(2,1)S(1)}, u32[]{:S(2)}, u32[]{:S(2)}) %all-to-all-start.3) | async-done | bytes 458784 | tf_op jit(solution)/shard_map/all_to_all | solution.py:49
  116.2 2.7 %fusion.35 = bf16[128,1024]{1,0:T(8,128)(2,1)S(1)} fusion(bf16[128,1792]{1,0:T(8,128)(2,1)S(1)} %bitcast.91, bf16[1,1792,1024]{2,1,0:T(8,128)(2,1)} %param.12), kind=kOutput, calls=%fused_computation.32 | convolution fusion | flops 469893120 | bytes 4390912 | tf_op jit(solution)/shard_map/dot_general | solution.py:68
  118.9 0.9 pad_maximum_fusion
  119.9 25.7 %reduce-scatter.2.cloned.1.call-done = bf16[32,3072]{1,0:T(8,128)(2,1)} async-done(((bf16[128,3072]{1,0:T(8,128)(2,1)}), bf16[32,3072]{1,0:T(8,128)(2,1)}) %reduce-scatter.2.cloned.1.call-update) | async-done | bytes 196624 | tf_op jit(solution)/shard_map/reduce_scatter | solution.py:63
  145.6 1.0 convert_element_type.62
  146.6 9.1 %all_gather.10 = bf16[128,1024]{1,0:T(8,128)(2,1)S(1)} all-gather(bf16[32,1024]{1,0:T(8,128)(2,1)S(1)} %get-tuple-element.5), channel_id=1, replica_groups=mesh['dp'=4,'expert'=8] {'dp'}, dimensions={0}, use_global_device_ids=true | all-gather | bytes 327680 | tf_op jit(solution)/shard_map/all_gather | solution.py:88
  155.7 8.4 %all_gather.9 = bf16[128,1024]{1,0:T(8,128)(2,1)S(1)} all-gather(bf16[32,1024]{1,0:T(8,128)(2,1)S(1)} %get-tuple-element.6), channel_id=1, replica_groups=mesh['dp'=4,'expert'=8] {'dp'}, dimensions={0}, use_global_device_ids=true | all-gather | bytes 327680 | tf_op jit(solution)/shard_map/all_gather | solution.py:87
  164.1 9.0 %all_gather.11 = bf16[128,1024]{1,0:T(8,128)(2,1)S(1)} all-gather(bf16[32,1024]{1,0:T(8,128)(2,1)S(1)} %get-tuple-element.7), channel_id=1, replica_groups=mesh['dp'=4,'expert'=8] {'dp'}, dimensions={0}, use_global_device_ids=true | all-gather | bytes 327680 | tf_op jit(solution)/shard_map/all_gather | solution.py:89
  173.2 3.4 %fusion.21 = bf16[128,1792]{1,0:T(8,128)(2,1)S(1)} fusion(bf16[128,1024]{1,0:T(8,128)(2,1)S(1)} %all_gather.9, bf16[1,1792,1024]{2,1,0:T(8,128)(2,1)} %param.12), kind=kOutput, calls=%fused_computation.26 | convolution fusion | flops 469991424 | bytes 4390912 | tf_op jit(solution)/shard_map/dot_general | solution.py:10
  176.5 0.9 copy.80
  177.4 3.5 %all-to-all-start.4 = ((bf16[8,16,1792]{2,0,1:T(8,128)(2,1)}), bf16[8,16,1792]{2,0,1:T(8,128)(2,1)S(1)}, u32[]{:S(2)}, u32[]{:S(2)}) async-start(bf16[8,16,1792]{2,0,1:T(8,128)(2,1)} %copy.80), calls=%async_computation.5 | async-start | bytes 917504 | tf_op jit(solution)/shard_map/all_to_all | solution.py:105
  180.9 3.5 %fusion.7 = f32[128,1792]{1,0:T(8,128)S(1)} fusion(bf16[128,1024]{1,0:T(8,128)(2,1)S(1)} %all_gather.11, bf16[1,1792,1024]{2,1,0:T(8,128)(2,1)} %param.11), kind=kOutput, calls=%fused_computation.14 | convolution fusion | flops 469762048 | bytes 4849664 | tf_op jit(solution)/shard_map/dot_general | solution.py:10
  184.5 1.4 fusion.24
  185.8 0.9 copy.84
  186.7 0.6 all-to-all-done.4
  187.4 3.5 %all-to-all-start.6 = ((bf16[8,16,1792]{2,0,1:T(8,128)(2,1)}), bf16[8,16,1792]{2,0,1:T(8,128)(2,1)S(1)}, u32[]{:S(2)}, u32[]{:S(2)}) async-start(bf16[8,16,1792]{2,0,1:T(8,128)(2,1)} %copy.84), calls=%async_computation.7 | async-start | bytes 917504 | tf_op jit(solution)/shard_map/all_to_all | solution.py:112
  190.9 0.4 copy.91
  191.2 0.9 reshape.50
  192.2 4.9 %all-to-all-done.6 = bf16[8,16,1792]{2,0,1:T(8,128)(2,1)S(1)} async-done(((bf16[8,16,1792]{2,0,1:T(8,128)(2,1)}), bf16[8,16,1792]{2,0,1:T(8,128)(2,1)S(1)}, u32[]{:S(2)}, u32[]{:S(2)}) %all-to-all-start.6) | async-done | bytes 458784 | tf_op jit(solution)/shard_map/all_to_all | solution.py:112
  197.1 4.6 %all-to-all-start.5 = ((bf16[8,4,7168]{2,1,0:T(4,128)(2,1)}), bf16[8,4,7168]{2,1,0:T(4,128)(2,1)S(1)}, u32[]{:S(2)}, u32[]{:S(2)}) async-start(bf16[8,4,7168]{2,1,0:T(4,128)(2,1)} %reshape.50), calls=%async_computation.6 | async-start | bytes 917504 | tf_op jit(solution)/shard_map/all_to_all | solution.py:104
  202.1 0.9 all_to_all.82
  203.0 12.6 %all-to-all-done.5 = bf16[8,4,7168]{2,1,0:T(4,128)(2,1)S(1)} async-done(((bf16[8,4,7168]{2,1,0:T(4,128)(2,1)}), bf16[8,4,7168]{2,1,0:T(4,128)(2,1)S(1)}, u32[]{:S(2)}, u32[]{:S(2)}) %all-to-all-start.5) | async-done | bytes 458784 | tf_op jit(solution)/shard_map/all_to_all | solution.py:104
  215.7 4.1 %all-to-all-start.7 = ((bf16[8,4,7168]{2,1,0:T(4,128)(2,1)}), bf16[8,4,7168]{2,1,0:T(4,128)(2,1)}, u32[]{:S(2)}, u32[]{:S(2)}) async-start(bf16[8,4,7168]{2,1,0:T(4,128)(2,1)} %all_to_all.82), calls=%async_computation.8 | async-start | bytes 917504 | tf_op jit(solution)/shard_map/all_to_all | solution.py:111
  219.8 3.0 %fusion.17 = bf16[1,1792,1024]{2,1,0:T(8,128)(2,1)} fusion(bf16[128,1792]{1,0:T(8,128)(2,1)S(1)} %bitcast.92, bf16[128,1024]{1,0:T(8,128)(2,1)S(1)} %all_gather.9), kind=kOutput, calls=%fused_computation.24 | convolution fusion | flops 471597056 | bytes 4390912 | tf_op jit(solution)/shard_map/dot_general | solution.py:16
  222.8 3.0 %fusion.15 = bf16[1,1792,1024]{2,1,0:T(8,128)(2,1)} fusion(bf16[128,1792]{1,0:T(8,128)(2,1)S(1)} %bitcast.89, bf16[128,1024]{1,0:T(8,128)(2,1)S(1)} %all_gather.10), kind=kOutput, calls=%fused_computation.22 | convolution fusion | flops 471597056 | bytes 4390912 | tf_op jit(solution)/shard_map/dot_general | solution.py:16
  225.7 3.0 %fusion.16 = bf16[1,1792,1024]{2,1,0:T(8,128)(2,1)} fusion(bf16[128,1792]{1,0:T(8,128)(2,1)S(1)} %bitcast.90, bf16[128,1024]{1,0:T(8,128)(2,1)S(1)} %all_gather.11), kind=kOutput, calls=%fused_computation.23 | convolution fusion | flops 471597056 | bytes 4390912 | tf_op jit(solution)/shard_map/dot_general | solution.py:16
  228.7 2.9 %fusion = bf16[128,7168]{1,0:T(8,128)(2,1)} fusion(bf16[8,4,7168]{2,1,0:T(4,128)(2,1)S(1)} %all-to-all-done.5, f32[8,4]{0,1:T(4,128)S(1)} %select_reduce_fusion.1, s32[128,8]{0,1:T(8,128)S(1)} %copy.71, pred[128,8]{0,1:T(8,128)(4,1)S(1)} %copy.70), kind=kOutput, calls=%fused_computation.2 | convolution fusion | flops 353705984 | bytes 2299008 | tf_op jit(solution)/shard_map/tjc,jcd->td/dot_general | solution.py:122
  231.7 2.1 all-to-all-done.7
  233.7 2.9 %fusion.1 = bf16[128,7168]{1,0:T(8,128)(2,1)} fusion(bf16[8,4,7168]{2,1,0:T(4,128)(2,1)} %all-to-all-done.7, s32[128,8]{0,1:T(8,128)S(1)} %copy.71, pred[128,8]{0,1:T(8,128)(4,1)S(1)} %copy.70), kind=kOutput, calls=%fused_computation.3 | convolution fusion | flops 59645952 | bytes 2298880 | tf_op jit(solution)/shard_map/tjc,jcd->td/dot_general | solution.py:125
  (29 shorter events, 1.6 us)
Async XLA Ops:
  7.2 1.5 copy-start
  16.3 15.4 %copy-start.5 = (s32[128,8]{0,1:T(8,128)S(1)}, s32[128,8]{0,1:T(8,128)}, u32[]{:S(2)}) copy-start(s32[128,8]{0,1:T(8,128)} %param.8) | copy-start | bytes 12292
  16.3 15.4 %copy-start.6 = (f32[128,8]{0,1:T(8,128)S(1)}, f32[128,8]{0,1:T(8,128)}, u32[]{:S(2)}) copy-start(f32[128,8]{0,1:T(8,128)} %param.9) | copy-start | bytes 12292
  16.3 15.5 %copy-start.4 = (bf16[128,7168]{1,0:T(8,128)(2,1)S(1)}, bf16[128,7168]{1,0:T(8,128)(2,1)}, u32[]{:S(2)}) copy-start(bf16[128,7168]{1,0:T(8,128)(2,1)} %param.13) | copy-start | bytes 5505028
  26.5 23.0 %all-to-all-start = ((bf16[4,2,28672]{2,1,0:T(2,128)(2,1)}), bf16[4,2,28672]{2,1,0:T(2,128)(2,1)S(1)}, u32[]{:S(2)}, u32[]{:S(2)}) async-start(bf16[4,2,28672]{2,1,0:T(2,128)(2,1)} %reshape.53), calls=%async_computation | async-start | bytes 917504 | tf_op jit(solution)/shard_map/all_to_all | solution.py:43
  49.5 23.5 %all-to-all-start.2 = ((bf16[4,2,28672]{2,1,0:T(2,128)(2,1)}), bf16[4,2,28672]{2,1,0:T(2,128)(2,1)S(1)}, u32[]{:S(2)}, u32[]{:S(2)}) async-start(bf16[4,2,28672]{2,1,0:T(2,128)(2,1)} %reshape.51), calls=%async_computation.2 | async-start | bytes 917504 | tf_op jit(solution)/shard_map/all_to_all | solution.py:50
  73.0 24.2 %all-to-all-start.1 = ((bf16[8,16,1792]{2,1,0:T(8,128)(2,1)}), bf16[8,16,1792]{2,1,0:T(8,128)(2,1)S(1)}, u32[]{:S(2)}, u32[]{:S(2)}) async-start(bf16[8,16,1792]{2,1,0:T(8,128)(2,1)} %copy.75), calls=%async_computation.1 | async-start | bytes 917504 | tf_op jit(solution)/shard_map/all_to_all | solution.py:42
  97.2 19.0 %all-to-all-start.3 = ((bf16[8,16,1792]{2,1,0:T(8,128)(2,1)}), bf16[8,16,1792]{2,1,0:T(8,128)(2,1)S(1)}, u32[]{:S(2)}, u32[]{:S(2)}) async-start(bf16[8,16,1792]{2,1,0:T(8,128)(2,1)} %copy.79), calls=%async_computation.3 | async-start | bytes 917504 | tf_op jit(solution)/shard_map/all_to_all | solution.py:49
  102.3 43.3 %reduce-scatter.2.cloned.1.call-start = ((), (), s32[]{:S(2)}) async-start(), calls=%async_computation.9 | async-start | bytes 983040 | tf_op jit(solution)/shard_map/reduce_scatter | solution.py:63
  102.3 3.1 %copy-start.2 = (bf16[1,1792,1024]{2,1,0:T(8,128)(2,1)S(1)}, bf16[1,1792,1024]{2,1,0:T(8,128)(2,1)}, u32[]{:S(2)}) copy-start(bf16[1,1792,1024]{2,1,0:T(8,128)(2,1)} %param.10) | copy-start | bytes 11010052
  177.4 9.9 %all-to-all-start.4 = ((bf16[8,16,1792]{2,0,1:T(8,128)(2,1)}), bf16[8,16,1792]{2,0,1:T(8,128)(2,1)S(1)}, u32[]{:S(2)}, u32[]{:S(2)}) async-start(bf16[8,16,1792]{2,0,1:T(8,128)(2,1)} %copy.80), calls=%async_computation.5 | async-start | bytes 917504 | tf_op jit(solution)/shard_map/all_to_all | solution.py:105
  180.9 3.5 %copy-start.3 = (bf16[1,1792,1024]{2,1,0:T(8,128)(2,1)S(1)}, bf16[1,1792,1024]{2,1,0:T(8,128)(2,1)}, u32[]{:S(2)}) copy-start(bf16[1,1792,1024]{2,1,0:T(8,128)(2,1)} %param.10) | copy-start | bytes 11010052
  187.4 9.8 %all-to-all-start.6 = ((bf16[8,16,1792]{2,0,1:T(8,128)(2,1)}), bf16[8,16,1792]{2,0,1:T(8,128)(2,1)S(1)}, u32[]{:S(2)}, u32[]{:S(2)}) async-start(bf16[8,16,1792]{2,0,1:T(8,128)(2,1)} %copy.84), calls=%async_computation.7 | async-start | bytes 917504 | tf_op jit(solution)/shard_map/all_to_all | solution.py:112
  197.1 18.5 %all-to-all-start.5 = ((bf16[8,4,7168]{2,1,0:T(4,128)(2,1)}), bf16[8,4,7168]{2,1,0:T(4,128)(2,1)S(1)}, u32[]{:S(2)}, u32[]{:S(2)}) async-start(bf16[8,4,7168]{2,1,0:T(4,128)(2,1)} %reshape.50), calls=%async_computation.6 | async-start | bytes 917504 | tf_op jit(solution)/shard_map/all_to_all | solution.py:104
  215.7 18.1 %all-to-all-start.7 = ((bf16[8,4,7168]{2,1,0:T(4,128)(2,1)}), bf16[8,4,7168]{2,1,0:T(4,128)(2,1)}, u32[]{:S(2)}, u32[]{:S(2)}) async-start(bf16[8,4,7168]{2,1,0:T(4,128)(2,1)} %all_to_all.82), calls=%async_computation.8 | async-start | bytes 917504 | tf_op jit(solution)/shard_map/all_to_all | solution.py:111
  222.8 13.9 %copy-start.1 = (bf16[128,7168]{1,0:T(8,128)(2,1)S(1)}, bf16[128,7168]{1,0:T(8,128)(2,1)}, u32[]{:S(2)}) copy-start(bf16[128,7168]{1,0:T(8,128)(2,1)} %param.7) | copy-start | bytes 5505028
Sparse Core Ops, SparseCore 0:
  120.0 25.5 reduce-scatter.1
where the time goes:
time: 245 us; the launch traced here: 243 us
  local copies, waits for them, and re-layouts  78.5 us (32%)
  waiting for transfers between devices  56.1 us (23%)
  starting transfers between devices  35.1 us (14%)
  matrix products  29.9 us (12%)
  blocking collectives  26.5 us (11%)
  between operations  14.2 us (6%)
  other arithmetic  3.11 us (1%)
    unnamed x18, local copies, waits for them, and re-layouts  40.4 us
    reduce_scatter x1, waiting for transfers between devices, body(): lax.psum_scatter(jnp.concatenate([jnp.dot(row_block, gate_mat, preferred_...  25.7 us
    all_to_all x1, waiting for transfers between devices, body(): lax.all_to_all(lax.all_to_all(out_rows.reshape(layout), 'dp', split_axis=...  12.6 us
    all_to_all x1, waiting for transfers between devices, body(): lax.all_to_all(lax.all_to_all(send_grads, 'dp', split_axis=2, concat_axis...  10.1 us
    all_to_all x2, local copies, waits for them, and re-layouts, body(): lax.all_to_all(send_rows, 'dp', split_axis=2, concat_axis=1, tiled=True)  9.54 us
    all_to_all x2, local copies, waits for them, and re-layouts, body(): lax.all_to_all(send_grads, 'dp', split_axis=2, concat_axis=1, tiled=True)  9.54 us
    all_gather x1, blocking collectives, body(): gate_part = lax.all_gather(gate_grad, 'dp', axis=0, tiled=True)  9.05 us
    all_gather x1, blocking collectives, body(): up_part = lax.all_gather(up_grad, 'dp', axis=0, tiled=True)  9.04 us
  transfers between devices with their start and end apart: 9, of which 6 were waited for; matrix products, arithmetic and copies ran while one was open for 33% of the time, Pallas kernels for 0%

commit v1 on v0

--- a/solution.py
+++ b/solution.py
@@ -4,6 +4,30 @@
 from jax.sharding import PartitionSpec as P
 
 CAP = 4
+
+
+def in_blocks(x, dim, length):
+    lengths = x.shape
+    blocks = x.reshape(*lengths[:dim], length, lengths[dim] // length, *lengths[dim + 1 :])
+    return jnp.moveaxis(blocks, dim, 0)
+
+
+def joined_along(blocks, dim):
+    lengths = list(blocks.shape[1:])
+    lengths[dim] *= blocks.shape[0]
+    return jnp.moveaxis(blocks, 0, dim).reshape(lengths)
+
+
+def rotated_exchange(x, axis, split_dim, concat_dim):
+    size, index = (lax.axis_size(axis), lax.axis_index(axis))
+    pieces = in_blocks(x, split_dim, size)
+    out = pieces
+    for step in range(1, size):
+        target, source = ((index + step) % size, (index - step) % size)
+        sent = lax.dynamic_index_in_dim(pieces, target, 0)
+        other = lax.ppermute(sent, axis, [(i, (i + step) % size) for i in range(size)])
+        out = lax.dynamic_update_slice_in_dim(out, other, source, axis=0)
+    return joined_along(out, concat_dim)
 
 
 def contract_last(left, right):
@@ -47,7 +71,7 @@
             tiled=True,
         ),
         lax.all_to_all(
-            lax.all_to_all(send_grads, "dp", split_axis=2, concat_axis=1, tiled=True),
+            rotated_exchange(send_grads, "dp", 2, 1),
             "expert",
             split_axis=0,
             concat_axis=0,

time: 245 us -> 221 us (0.902)
  local copies, waits for them, and re-layouts: 78.5 us -> 51.5 us
  waiting for transfers between devices: 56.1 us -> 52.5 us
    unnamed x18 -> x8, local copies, waits for them, and re-layouts: 40.4 us -> 20.2 us
    all_to_all x1, waiting for transfers between devices: 0.01 us -> 11.2 us  [body(): lax.all_to_all(lax.all_to_all(send_rows, 'dp', split_axis=2, concat_axis=...]
    all_to_all x1, waiting for transfers between devices: 12.6 us -> 2.06 us  [body(): lax.all_to_all(lax.all_to_all(out_rows.reshape(layout), 'dp', split_axis=...]
    all_to_all x2 -> x1, waiting for transfers between devices: 10.1 us -> 0.01 us  [body(): lax.all_to_all(rotated_exchange(send_grads, 'dp', 2, 1), 'expert', split_...]
    all_to_all x2 -> x0, local copies, waits for them, and re-layouts: 9.54 us -> none  [body(): lax.all_to_all(send_grads, 'dp', split_axis=2, concat_axis=1, tiled=True)]
    all_to_all x1, waiting for transfers between devices: 2.05 us -> 9.93 us  [body(): lax.all_to_all(lax.all_to_all(input_rows.reshape(layout), 'dp', split_axi...]
    convert_element_type x1 -> x0, local copies, waits for them, and re-layouts: 7.2 us -> none  [body(): send_grads = (slot_gate[:, :, None] * picked).astype(jnp.bfloat16)]
    ppermute x0 -> x3, starting transfers between devices: none -> 5.92 us  [rotated_exchange(): lax.ppermute(sent, axis, [(i, (i + step) % size) for i in range(size)])]
  transfers between devices with their start and end apart: 9 -> 11, of which waited for: 6 -> 6; matrix products, arithmetic and copies ran while one was open for 33% -> 31% of each run, Pallas kernels for 0% -> 0%
where the time goes in v1:
time: 221 us; the launch traced here: 219 us
  waiting for transfers between devices  52.5 us (24%)
  local copies, waits for them, and re-layouts  51.5 us (23%)
  starting transfers between devices  36.5 us (17%)
  matrix products  32.3 us (15%)
  blocking collectives  27.6 us (12%)
  between operations  14.3 us (6%)
  other arithmetic  4.6 us (2%)
    reduce_scatter x1, waiting for transfers between devices, body(): lax.psum_scatter(jnp.concatenate([jnp.dot(row_block, gate_mat, preferred_...  24.3 us
    unnamed x8, local copies, waits for them, and re-layouts  20.2 us
    all_to_all x1, waiting for transfers between devices, body(): lax.all_to_all(lax.all_to_all(send_rows, 'dp', split_axis=2, concat_axis=...  11.2 us
    all_gather x1, blocking collectives, body(): hidden_part = lax.all_gather(hidden, 'dp', axis=0, tiled=True)  10.6 us
    all_to_all x1, waiting for transfers between devices, body(): lax.all_to_all(lax.all_to_all(input_rows.reshape(layout), 'dp', split_axi...  9.93 us
    all_to_all x2, local copies, waits for them, and re-layouts, body(): lax.all_to_all(send_rows, 'dp', split_axis=2, concat_axis=1, tiled=True)  9.54 us
    all_gather x1, blocking collectives, body(): up_part = lax.all_gather(up_grad, 'dp', axis=0, tiled=True)  9.04 us
    dot_general x3, matrix products, contract_first(): lax.dot_general(left, right, (((0,), (0,)), ((), ())), preferred_element_...  8.94 us
  transfers between devices with their start and end apart: 11, of which 6 were waited for; matrix products, arithmetic and copies ran while one was open for 31% of the time, Pallas kernels for 0%

profile of v1, /device:TPU:0, one launch (start us, length us, event | category | flops | bytes accessed | tf_op | source)
XLA Modules:
  0.0 219.3 jit_solution(5409831113310534493)
XLA Ops:
  7.2 0.8 fusion.44
  10.4 3.0 %collective-permute-start = (bf16[1,8,4,1792]{3,1,2,0:T(8,128)(2,1)}, bf16[1,8,4,1792]{3,1,2,0:T(8,128)(2,1)}, u32[]{:S(2)}, u32[]{:S(2)}) collective-permute-start(bf16[1,8,4,1792]{3,1,2,0:T(8,128)(2,1)} %get-tuple-element.7), channel_id=1, source_target_pairs={{0,8},{8,16},{16,24},{24,0},{1,9},{9,17},{17,25},{25,1},{2,10},{10... | collective-permute-start | bytes 344072 | tf_op jit(solution)/shard_map/ppermute | solution.py:28
  13.4 1.5 collective-permute-start.1
  14.9 1.4 collective-permute-start.2
  16.4 1.9 convolution_convert_fusion
  18.2 7.2 %copy.70 = bf16[8,4,7168]{0,1,2:T(4,128)(2,1)} copy(bf16[8,4,7168]{2,0,1:T(8,128)(2,1)S(1)} %convolution_convert_fusion) | data formatting | bytes 917504 | tf_op jit(solution)/shard_map/convert_element_type | solution.py:62
  25.4 10.1 %reshape.62 = bf16[4,2,28672]{2,1,0:T(2,128)(2,1)} reshape(bf16[7168,4,8]{2,1,0:T(4,128)(2,1)} %bitcast.89) | data formatting | bytes 917504
  35.5 3.5 %all-to-all-start = ((bf16[4,2,28672]{2,1,0:T(2,128)(2,1)}), bf16[4,2,28672]{2,1,0:T(2,128)(2,1)S(1)}, u32[]{:S(2)}, u32[]{:S(2)}) async-start(bf16[4,2,28672]{2,1,0:T(2,128)(2,1)} %reshape.62), calls=%async_computation | async-start | bytes 917504 | tf_op jit(solution)/shard_map/all_to_all | solution.py:67
  39.1 0.9 constant_dynamic-update-slice_fusion.2
  40.0 0.9 constant_dynamic-update-slice_fusion.1
  40.9 0.9 constant_dynamic-update-slice_fusion
  41.9 0.8 copy.75
  42.7 3.0 %all-to-all-done = bf16[4,2,28672]{2,1,0:T(2,128)(2,1)S(1)} async-done(((bf16[4,2,28672]{2,1,0:T(2,128)(2,1)}), bf16[4,2,28672]{2,1,0:T(2,128)(2,1)S(1)}, u32[]{:S(2)}, u32[]{:S(2)}) %all-to-all-start) | async-done | bytes 458784 | tf_op jit(solution)/shard_map/all_to_all | solution.py:67
  45.7 4.9 %all-to-all-start.2 = ((bf16[8,16,1792]{2,1,0:T(8,128)(2,1)}), bf16[8,16,1792]{2,1,0:T(8,128)(2,1)S(1)}, u32[]{:S(2)}, u32[]{:S(2)}) async-start(bf16[8,16,1792]{2,1,0:T(8,128)(2,1)} %copy.75), calls=%async_computation.2 | async-start | bytes 917504 | tf_op jit(solution)/shard_map/all_to_all | solution.py:73
  50.6 9.8 %reshape.63 = bf16[7168,4,8]{2,1,0:T(4,128)(2,1)} reshape(bf16[4,2,28672]{2,1,0:T(2,128)(2,1)S(1)} %all-to-all-done) | data formatting | bytes 917504
  60.3 8.7 %copy.72 = bf16[8,4,4,1792]{3,0,2,1:T(8,128)(2,1)S(1)} copy(bf16[8,4,4,1792]{0,2,3,1:T(4,128)(2,1)} %bitcast.90) | data formatting | bytes 917504 | tf_op jit(solution)/shard_map/all_to_all | solution.py:67
  69.1 0.8 copy.73
  69.9 5.1 %all-to-all-start.1 = ((bf16[8,16,1792]{2,1,0:T(8,128)(2,1)}), bf16[8,16,1792]{2,1,0:T(8,128)(2,1)S(1)}, u32[]{:S(2)}, u32[]{:S(2)}) async-start(bf16[8,16,1792]{2,1,0:T(8,128)(2,1)} %copy.73), calls=%async_computation.1 | async-start | bytes 917504 | tf_op jit(solution)/shard_map/all_to_all | solution.py:66
  75.0 2.7 %fusion.35 = bf16[128,1024]{1,0:T(8,128)(2,1)S(1)} fusion(bf16[128,1792]{1,0:T(8,128)(2,1)S(1)} %bitcast.95, bf16[1,1792,1024]{2,1,0:T(8,128)(2,1)} %param.12), kind=kOutput, calls=%fused_computation.32 | convolution fusion | flops 469893120 | bytes 4390912 | tf_op jit(solution)/shard_map/dot_general | solution.py:92
  77.7 11.2 %all-to-all-done.1 = bf16[8,16,1792]{2,1,0:T(8,128)(2,1)S(1)} async-done(((bf16[8,16,1792]{2,1,0:T(8,128)(2,1)}), bf16[8,16,1792]{2,1,0:T(8,128)(2,1)S(1)}, u32[]{:S(2)}, u32[]{:S(2)}) %all-to-all-start.1) | async-done | bytes 458784 | tf_op jit(solution)/shard_map/all_to_all | solution.py:66
  88.9 2.8 %fusion.29 = bf16[128,1024]{1,0:T(8,128)(2,1)S(1)} fusion(bf16[128,1792]{1,0:T(8,128)(2,1)S(1)} %bitcast.91, bf16[1,1792,1024]{2,1,0:T(8,128)(2,1)} %param.10), kind=kOutput, calls=%fused_computation.30 | convolution fusion | flops 469893120 | bytes 4390912 | tf_op jit(solution)/shard_map/dot_general | solution.py:90
  92.7 0.9 pad_maximum_fusion
  93.7 24.3 %reduce-scatter.2.cloned.1.call-done = bf16[32,3072]{1,0:T(8,128)(2,1)} async-done(((bf16[128,3072]{1,0:T(8,128)(2,1)}), bf16[32,3072]{1,0:T(8,128)(2,1)}) %reduce-scatter.2.cloned.1.call-update) | async-done | bytes 196624 | tf_op jit(solution)/shard_map/reduce_scatter | solution.py:87
  118.0 1.1 convert_element_type.62
  119.8 9.0 %all_gather.11 = bf16[128,1024]{1,0:T(8,128)(2,1)S(1)} all-gather(bf16[32,1024]{1,0:T(8,128)(2,1)S(1)} %get-tuple-element.10), channel_id=1, replica_groups=mesh['dp'=4,'expert'=8] {'dp'}, dimensions={0}, use_global_device_ids=true | all-gather | bytes 327680 | tf_op jit(solution)/shard_map/all_gather | solution.py:113
  128.8 7.9 %all_gather.10 = bf16[128,1024]{1,0:T(8,128)(2,1)S(1)} all-gather(bf16[32,1024]{1,0:T(8,128)(2,1)S(1)} %get-tuple-element.8), channel_id=1, replica_groups=mesh['dp'=4,'expert'=8] {'dp'}, dimensions={0}, use_global_device_ids=true | all-gather | bytes 327680 | tf_op jit(solution)/shard_map/all_gather | solution.py:112
  136.7 3.4 %fusion.7 = f32[128,1792]{1,0:T(8,128)S(1)} fusion(bf16[128,1024]{1,0:T(8,128)(2,1)S(1)} %all_gather.11, bf16[1,1792,1024]{2,1,0:T(8,128)(2,1)} %param.11), kind=kOutput, calls=%fused_computation.14 | convolution fusion | flops 469762048 | bytes 4849664 | tf_op jit(solution)/shard_map/dot_general | solution.py:34
  140.1 1.3 fusion.24
  141.5 0.9 copy.80
  142.4 4.1 %all-to-all-start.5 = ((bf16[8,16,1792]{2,0,1:T(8,128)(2,1)}), bf16[8,16,1792]{2,0,1:T(8,128)(2,1)}, u32[]{:S(2)}, u32[]{:S(2)}) async-start(bf16[8,16,1792]{2,0,1:T(8,128)(2,1)} %copy.80), calls=%async_computation.6 | async-start | bytes 917504 | tf_op jit(solution)/shard_map/all_to_all | solution.py:136
  146.5 10.6 %all_gather.9 = bf16[128,1024]{1,0:T(8,128)(2,1)S(1)} all-gather(bf16[32,1024]{1,0:T(8,128)(2,1)} %get-tuple-element.9), channel_id=1, replica_groups=mesh['dp'=4,'expert'=8] {'dp'}, dimensions={0}, use_global_device_ids=true | all-gather | bytes 327680 | tf_op jit(solution)/shard_map/all_gather | solution.py:111
  157.2 3.4 %fusion.21 = bf16[128,1792]{1,0:T(8,128)(2,1)S(1)} fusion(bf16[128,1024]{1,0:T(8,128)(2,1)S(1)} %all_gather.9, bf16[1,1792,1024]{2,1,0:T(8,128)(2,1)} %param.12), kind=kOutput, calls=%fused_computation.26 | convolution fusion | flops 469991424 | bytes 4390912 | tf_op jit(solution)/shard_map/dot_general | solution.py:34
  160.5 0.9 copy.76
  161.4 4.3 %all-to-all-start.3 = ((bf16[8,16,1792]{2,0,1:T(8,128)(2,1)}), bf16[8,16,1792]{2,0,1:T(8,128)(2,1)}, u32[]{:S(2)}, u32[]{:S(2)}) async-start(bf16[8,16,1792]{2,0,1:T(8,128)(2,1)} %copy.76), calls=%async_computation.4 | async-start | bytes 917504 | tf_op jit(solution)/shard_map/all_to_all | solution.py:129
  165.7 2.1 copy.81
  167.9 2.0 all_to_all.65
  169.8 2.0 all-to-all-done.3
  171.9 4.6 %all-to-all-start.6 = ((bf16[8,4,7168]{2,1,0:T(4,128)(2,1)}), bf16[8,4,7168]{2,1,0:T(4,128)(2,1)}, u32[]{:S(2)}, u32[]{:S(2)}) async-start(bf16[8,4,7168]{2,1,0:T(4,128)(2,1)} %all_to_all.65), calls=%async_computation.7 | async-start | bytes 917504 | tf_op jit(solution)/shard_map/all_to_all | solution.py:135
  176.5 2.1 copy.85
  178.6 2.0 reshape.61
  180.6 9.9 %all-to-all-done.6 = bf16[8,4,7168]{2,1,0:T(4,128)(2,1)} async-done(((bf16[8,4,7168]{2,1,0:T(4,128)(2,1)}), bf16[8,4,7168]{2,1,0:T(4,128)(2,1)}, u32[]{:S(2)}, u32[]{:S(2)}) %all-to-all-start.6) | async-done | bytes 458784 | tf_op jit(solution)/shard_map/all_to_all | solution.py:135
  190.5 4.1 %all-to-all-start.4 = ((bf16[8,4,7168]{2,1,0:T(4,128)(2,1)}), bf16[8,4,7168]{2,1,0:T(4,128)(2,1)}, u32[]{:S(2)}, u32[]{:S(2)}) async-start(bf16[8,4,7168]{2,1,0:T(4,128)(2,1)} %reshape.61), calls=%async_computation.5 | async-start | bytes 917504 | tf_op jit(solution)/shard_map/all_to_all | solution.py:128
  194.6 3.0 %fusion.16 = bf16[1,1792,1024]{2,1,0:T(8,128)(2,1)} fusion(bf16[128,1792]{1,0:T(8,128)(2,1)S(1)} %bitcast.93, bf16[128,1024]{1,0:T(8,128)(2,1)S(1)} %all_gather.11), kind=kOutput, calls=%fused_computation.23 | convolution fusion | flops 471597056 | bytes 4390912 | tf_op jit(solution)/shard_map/dot_general | solution.py:40
  197.6 3.0 %fusion.15 = bf16[1,1792,1024]{2,1,0:T(8,128)(2,1)} fusion(bf16[128,1792]{1,0:T(8,128)(2,1)S(1)} %bitcast.94, bf16[128,1024]{1,0:T(8,128)(2,1)S(1)} %all_gather.10), kind=kOutput, calls=%fused_computation.22 | convolution fusion | flops 471597056 | bytes 4390912 | tf_op jit(solution)/shard_map/dot_general | solution.py:40
  200.6 3.0 %fusion.17 = bf16[1,1792,1024]{2,1,0:T(8,128)(2,1)} fusion(bf16[128,1792]{1,0:T(8,128)(2,1)S(1)} %bitcast.96, bf16[128,1024]{1,0:T(8,128)(2,1)S(1)} %all_gather.9), kind=kOutput, calls=%fused_computation.24 | convolution fusion | flops 471597056 | bytes 4390912 | tf_op jit(solution)/shard_map/dot_general | solution.py:40
  203.6 2.9 %fusion.1 = bf16[128,7168]{1,0:T(8,128)(2,1)} fusion(bf16[8,4,7168]{2,1,0:T(4,128)(2,1)} %all-to-all-done.6, s32[128,8]{0,1:T(8,128)S(1)} %copy.69, pred[128,8]{0,1:T(8,128)(4,1)S(1)} %copy.68), kind=kOutput, calls=%fused_computation.3 | convolution fusion | flops 59645952 | bytes 2298880 | tf_op jit(solution)/shard_map/tjc,jcd->td/dot_general | solution.py:149
  206.5 2.1 all-to-all-done.4
  208.5 3.9 %fusion = bf16[128,7168]{1,0:T(8,128)(2,1)} fusion(bf16[8,4,7168]{2,1,0:T(4,128)(2,1)} %all-to-all-done.4, f32[8,4]{0,1:T(4,128)S(1)} %select_reduce_fusion.1, s32[128,8]{0,1:T(8,128)S(1)} %copy.69, pred[128,8]{0,1:T(8,128)(4,1)S(1)} %copy.68), kind=kOutput, calls=%fused_computation.2 | convolution fusion | flops 353705984 | bytes 2299008 | tf_op jit(solution)/shard_map/tjc,jcd->td/dot_general | solution.py:146
  (26 shorter events, 4.1 us)
Async XLA Ops:
  7.2 2.2 copy-start
  10.4 28.7 %collective-permute-start = (bf16[1,8,4,1792]{3,1,2,0:T(8,128)(2,1)}, bf16[1,8,4,1792]{3,1,2,0:T(8,128)(2,1)}, u32[]{:S(2)}, u32[]{:S(2)}) collective-permute-start(bf16[1,8,4,1792]{3,1,2,0:T(8,128)(2,1)} %get-tuple-element.7), channel_id=1, source_target_pairs={{0,8},{8,16},{16,24},{24,0},{1,9},{9,17},{17,25},{25,1},{2,10},{10... | collective-permute-start | bytes 344072 | tf_op jit(solution)/shard_map/ppermute | solution.py:28
  13.4 26.6 %collective-permute-start.1 = (bf16[1,8,4,1792]{3,1,2,0:T(8,128)(2,1)S(1)}, bf16[1,8,4,1792]{3,1,2,0:T(8,128)(2,1)}, u32[]{:S(2)}, u32[]{:S(2)}) collective-permute-start(bf16[1,8,4,1792]{3,1,2,0:T(8,128)(2,1)S(1)} %get-tuple-element.6), channel_id=1, source_target_pairs={{0,16},{8,24},{16,0},{24,8},{1,17},{9,25},{17,1},{25,9},{2,18},{10... | collective-permute-start | bytes 344072 | tf_op jit(solution)/shard_map/ppermute | solution.py:28
  14.9 26.0 %collective-permute-start.2 = (bf16[1,8,4,1792]{3,1,2,0:T(8,128)(2,1)S(1)}, bf16[1,8,4,1792]{3,1,2,0:T(8,128)(2,1)}, u32[]{:S(2)}, u32[]{:S(2)}) collective-permute-start(bf16[1,8,4,1792]{3,1,2,0:T(8,128)(2,1)S(1)} %get-tuple-element.5), channel_id=1, source_target_pairs={{0,24},{8,0},{16,8},{24,16},{1,25},{9,1},{17,9},{25,17},{2,26},{10... | collective-permute-start | bytes 344072 | tf_op jit(solution)/shard_map/ppermute | solution.py:28
  35.5 10.2 %all-to-all-start = ((bf16[4,2,28672]{2,1,0:T(2,128)(2,1)}), bf16[4,2,28672]{2,1,0:T(2,128)(2,1)S(1)}, u32[]{:S(2)}, u32[]{:S(2)}) async-start(bf16[4,2,28672]{2,1,0:T(2,128)(2,1)} %reshape.62), calls=%async_computation | async-start | bytes 917504 | tf_op jit(solution)/shard_map/all_to_all | solution.py:67
  45.7 24.2 %all-to-all-start.2 = ((bf16[8,16,1792]{2,1,0:T(8,128)(2,1)}), bf16[8,16,1792]{2,1,0:T(8,128)(2,1)S(1)}, u32[]{:S(2)}, u32[]{:S(2)}) async-start(bf16[8,16,1792]{2,1,0:T(8,128)(2,1)} %copy.75), calls=%async_computation.2 | async-start | bytes 917504 | tf_op jit(solution)/shard_map/all_to_all | solution.py:73
  69.9 19.0 %all-to-all-start.1 = ((bf16[8,16,1792]{2,1,0:T(8,128)(2,1)}), bf16[8,16,1792]{2,1,0:T(8,128)(2,1)S(1)}, u32[]{:S(2)}, u32[]{:S(2)}) async-start(bf16[8,16,1792]{2,1,0:T(8,128)(2,1)} %copy.73), calls=%async_computation.1 | async-start | bytes 917504 | tf_op jit(solution)/shard_map/all_to_all | solution.py:66
  75.0 43.0 %reduce-scatter.2.cloned.1.call-start = ((), (), s32[]{:S(2)}) async-start(), calls=%async_computation.8 | async-start | bytes 983040 | tf_op jit(solution)/shard_map/reduce_scatter | solution.py:87
  88.9 3.1 %copy-start.1 = (bf16[1,1792,1024]{2,1,0:T(8,128)(2,1)S(1)}, bf16[1,1792,1024]{2,1,0:T(8,128)(2,1)}, u32[]{:S(2)}) copy-start(bf16[1,1792,1024]{2,1,0:T(8,128)(2,1)} %param.11) | copy-start | bytes 11010052
  118.0 22.2 %copy-start.2 = (bf16[1,1792,1024]{2,1,0:T(8,128)(2,1)S(1)}, bf16[1,1792,1024]{2,1,0:T(8,128)(2,1)}, u32[]{:S(2)}) copy-start(bf16[1,1792,1024]{2,1,0:T(8,128)(2,1)} %param.10) | copy-start | bytes 11010052
  142.4 19.1 %all-to-all-start.5 = ((bf16[8,16,1792]{2,0,1:T(8,128)(2,1)}), bf16[8,16,1792]{2,0,1:T(8,128)(2,1)}, u32[]{:S(2)}, u32[]{:S(2)}) async-start(bf16[8,16,1792]{2,0,1:T(8,128)(2,1)} %copy.80), calls=%async_computation.6 | async-start | bytes 917504 | tf_op jit(solution)/shard_map/all_to_all | solution.py:136
  161.4 10.4 %all-to-all-start.3 = ((bf16[8,16,1792]{2,0,1:T(8,128)(2,1)}), bf16[8,16,1792]{2,0,1:T(8,128)(2,1)}, u32[]{:S(2)}, u32[]{:S(2)}) async-start(bf16[8,16,1792]{2,0,1:T(8,128)(2,1)} %copy.76), calls=%async_computation.4 | async-start | bytes 917504 | tf_op jit(solution)/shard_map/all_to_all | solution.py:129
  171.9 18.6 %all-to-all-start.6 = ((bf16[8,4,7168]{2,1,0:T(4,128)(2,1)}), bf16[8,4,7168]{2,1,0:T(4,128)(2,1)}, u32[]{:S(2)}, u32[]{:S(2)}) async-start(bf16[8,4,7168]{2,1,0:T(4,128)(2,1)} %all_to_all.65), calls=%async_computation.7 | async-start | bytes 917504 | tf_op jit(solution)/shard_map/all_to_all | solution.py:135
  190.5 18.1 %all-to-all-start.4 = ((bf16[8,4,7168]{2,1,0:T(4,128)(2,1)}), bf16[8,4,7168]{2,1,0:T(4,128)(2,1)}, u32[]{:S(2)}, u32[]{:S(2)}) async-start(bf16[8,4,7168]{2,1,0:T(4,128)(2,1)} %reshape.61), calls=%async_computation.5 | async-start | bytes 917504 | tf_op jit(solution)/shard_map/all_to_all | solution.py:128
Sparse Core Ops, SparseCore 0:
  93.8 24.1 reduce-scatter.1
